TPU v7x, 256 devices: a whole 4x4x8 slice. The times are simulated.
256 devices in a mesh: mode: 16 (over x_hi, y, core), site: 16 (over z, x_lo).
Axes of the slice: x: 4 (x_hi: 2, x_lo: 2; x = x_hi * 2 + x_lo), y: 4, z: 8, core: 2. Of those that a mesh axis runs over, the one named last changes fastest.
Arguments:
- eigvecs: bfloat16 [2, 64, 3, 110592], P(None, 'mode', None, 'site'), may hold values from -6 to 6
- perams: bfloat16 [2, 16, 64, 64], replicated, may hold values from -0.75 to 0.75
- momenta: int32 [2, 3], replicated, may hold values from -2 to 2
- spins: int32 [16, 3], replicated, may hold values from 0 to 15
- pair_combs: int32 [16, 2], P('site'), may hold values from 0 to 15
- pair_moms: int32 [16, 2], P('site'), may hold values from 0 to 1
Outputs:
- exchange: float32 [16, 2, 64, 64], P('site', None, 'mode')
All inputs are finite; a program needn't handle non-finite values.
Results may differ from a plain program's by a relative error of at most 0.018.
Values may be sent and summed in bfloat16 or wider, within the bound.
No kernel may reach another device: no remote copies, remote signals or barrier semaphores. Data moves between devices by JAX's collectives and lax.ppermute only.
A program may use at most 64 MiB of HBM per device.

v0:
```python
import jax
import jax.numpy as jnp
from jax import lax
from jax.sharding import PartitionSpec as P

LAT = 48


def hartley(momenta, glob):
    coord_x = glob // (LAT * LAT)
    coord_y = glob // LAT % LAT
    coord_z = glob % LAT
    wave = (
        momenta[:, 0:1] * coord_x[None]
        + momenta[:, 1:2] * coord_y[None]
        + momenta[:, 2:3] * coord_z[None]
    ) % LAT
    theta = wave.astype(jnp.float32) * (2.0 * jnp.pi / LAT)
    return jnp.cos(theta) + jnp.sin(theta)


def body(eigvecs, perams, momenta, spins, pair_combs, pair_moms):
    nslice, mode_dev, _, site_dev = eigvecs.shape
    nmode = perams.shape[-1]
    nspin = perams.shape[1]
    ncomb = spins.shape[0]
    nmom = momenta.shape[0]
    comb_dev = ncomb // lax.axis_size("site")
    first_mode = lax.axis_index("mode") * mode_dev
    gathered = lax.all_gather(eigvecs, "mode", axis=1, tiled=True)
    glob = lax.axis_index("site") * site_dev + jnp.arange(site_dev, dtype=jnp.int32)
    phase = hartley(momenta, glob)

    def triplet_part(vectors):
        floats = vectors.astype(jnp.float32)
        own_modes = lax.dynamic_slice_in_dim(floats, first_mode, mode_dev, 0)
        left = own_modes[:, None]
        right = floats[None]
        cross_0 = left[:, :, 1] * right[:, :, 2] - left[:, :, 2] * right[:, :, 1]
        cross_1 = left[:, :, 2] * right[:, :, 0] - left[:, :, 0] * right[:, :, 2]
        cross_2 = left[:, :, 0] * right[:, :, 1] - left[:, :, 1] * right[:, :, 0]
        diquark = jnp.stack([cross_0, cross_1, cross_2], axis=2).astype(jnp.bfloat16)
        weighted = (phase[:, None, None, :] * floats[None]).astype(jnp.bfloat16)
        product = lax.dot_general(
            diquark.reshape(mode_dev * nmode, 3 * site_dev),
            weighted.reshape(nmom * nmode, 3 * site_dev),
            (((1,), (1,)), ((), ())),
            preferred_element_type=jnp.float32,
        )
        return product.reshape(mode_dev, nmode, nmom, nmode)

    partial_sums = lax.map(triplet_part, gathered)
    totals = lax.psum(partial_sums, "site")
    triplet = (totals * float(LAT) ** (-1.5)).astype(jnp.bfloat16)
    comb_ids = jnp.arange(ncomb, dtype=jnp.int32)
    mom_ids = jnp.arange(nmom, dtype=jnp.int32)
    spin_ids = jnp.arange(nspin, dtype=jnp.int32)
    own_spins = lax.dynamic_slice_in_dim(spins, lax.axis_index("site") * comb_dev, comb_dev, 0)
    picker = (own_spins[:, :, None] == spin_ids[None, None, :]).astype(jnp.bfloat16)
    chosen = jnp.einsum(
        "cks,tsmn->tckmn", picker, perams, preferred_element_type=jnp.float32
    ).astype(jnp.bfloat16)
    first = jnp.einsum(
        "tijpk,tcmk->tcijpm", triplet, chosen[:, :, 2], preferred_element_type=jnp.float32
    ).astype(jnp.bfloat16)
    second = jnp.einsum(
        "tcmj,tcijpk->itcpmk", chosen[:, :, 1], first, preferred_element_type=jnp.float32
    ).astype(jnp.bfloat16)
    rows_sel = chosen[:, :, 0]
    cols_sel = lax.dynamic_slice_in_dim(rows_sel, first_mode, mode_dev, 3)
    own_blocks = lax.psum_scatter(
        jnp.einsum("tcmi,itcpjk->mtcpjk", cols_sel, second, preferred_element_type=jnp.float32),
        "mode",
        scatter_dimension=0,
        tiled=True,
    ).astype(jnp.bfloat16)
    all_blocks = lax.all_gather(own_blocks, "site", axis=2, tiled=True)
    swapped = lax.all_to_all(all_blocks, "mode", split_axis=4, concat_axis=0, tiled=True)
    pick_left = (
        (pair_combs[:, 0][:, None, None] == comb_ids[None, :, None])
        & (pair_moms[:, 0][:, None, None] == mom_ids[None, None, :])
    ).astype(jnp.bfloat16)
    pick_right = (
        (pair_combs[:, 1][:, None, None] == comb_ids[None, :, None])
        & (pair_moms[:, 1][:, None, None] == mom_ids[None, None, :])
    ).astype(jnp.bfloat16)
    left_block = jnp.einsum(
        "qcp,itcpjk->qtijk", pick_left, all_blocks, preferred_element_type=jnp.float32
    ).astype(jnp.bfloat16)
    right_block = jnp.einsum(
        "qcp,mtcpnk->qtmnk", pick_right, swapped, preferred_element_type=jnp.float32
    ).astype(jnp.bfloat16)
    partial_corr = jnp.einsum(
        "qtijk,qtjil->qtkl", left_block, right_block, preferred_element_type=jnp.float32
    ) * (1.0 / nmode)
    return lax.psum_scatter(
        partial_corr.astype(jnp.bfloat16), "mode", scatter_dimension=2, tiled=True
    ).astype(jnp.float32)


def solution(mesh):
    placed = (P(None, "mode", None, "site"), P(), P(), P(), P("site", None), P("site", None))
    return jax.shard_map(
        body, mesh=mesh, in_specs=placed, out_specs=P("site", None, "mode", None), check_vma=False
    )
```

profile of v0, /device:TPU:38, one launch (start us, length us, event | category | flops | bytes accessed | tf_op | source)
XLA Modules:
  0.0 601.7 jit_solution(13482562929319963017)
XLA Ops:
  6.5 2.0 copy.22
  11.1 64.4 %all-gather.3.cloned.1.call-done = bf16[2,64,3,6912]{3,0,2,1:T(2,128)(2,1)} async-done(((bf16[2,4,3,6912]{3,0,2,1:T(2,128)(2,1)}), bf16[2,64,3,6912]{3,0,2,1:T(2,128)(2,1)}) %all-gather.3.cloned.1.call-update) | async-done | bytes 5308432 | tf_op jit(solution)/shard_map/all_gather | solution.py:30
  75.5 5.4 copy.23
  80.9 20.2 %while.13 = (s32[]{:T(128)}, f32[2,4,64,2,64]{4,2,3,1,0:T(8,128)S(1)}, bf16[2,64,3,6912]{3,1,2,0:T(8,128)(2,1)}, s32[]{:T(128)}, s32[6912]{0:T(1024)S(1)}, /*ind...) while((s32[]{:T(128)}, ...), condition=%wide.region_1.2_spmd.clone, body=%wide.region_0.1_spmd.clone.sunk | while | flops 1418867712 | bytes 57853072 | solution.py:52
  80.9 2.4 dynamic-slice_convert_fusion.3
  83.8 3.2 subtract_convert_fusion.4
  88.0 3.0 fusion.62
  91.0 2.4 dynamic-slice_convert_fusion.3
  93.9 3.2 subtract_convert_fusion.4
  98.1 3.0 fusion.62
  102.3 135.7 %all-reduce.3.cloned.1.call-done = f32[2,4,64,2,64]{4,2,3,1,0:T(8,128)} async-done(((f32[2,4,64,2,64]{4,2,3,1,0:T(8,128)}), f32[2,4,64,2,64]{4,2,3,1,0:T(8,128)}) %all-reduce.3.cloned.1.call-update) | async-done | bytes 262160 | tf_op jit(solution)/shard_map/psum | solution.py:53
  239.8 4.9 convolution_bitcast_fusion
  244.8 9.1 %copy.26 = f32[64,2,1,2,64,64]{5,4,3,2,1,0:T(8,128)} copy(f32[64,2,1,2,64,64]{0,5,4,3,1,2:T(8,128)} %convolution_bitcast_fusion) | data formatting | bytes 8388608 | tf_op jit(solution)/shard_map/tcmi,itcpjk->mtcpjk/transpose | solution.py:72
  254.1 109.6 %reduce-scatter.3.cloned.1.call-done = f32[4,2,1,2,64,64]{5,4,3,2,1,0:T(8,128)} async-done(((f32[64,2,1,2,64,64]{5,4,3,2,1,0:T(8,128)}), f32[4,2,1,2,64,64]{5,4,3,2,1,0:T(8,128)}) %reduce-scatter.3.cloned.1.call-update) | async-done | bytes 262160 | tf_op jit(solution)/shard_map/reduce_scatter | solution.py:71
  363.7 1.8 convert_bitcast_fusion
  365.5 99.9 %all-gather.5.cloned.1.call-done = bf16[4,2,16,2,64,64]{5,4,3,1,0,2:T(8,128)(2,1)} async-done(((bf16[4,2,1,2,64,64]{5,4,3,1,0,2:T(8,128)(2,1)}), bf16[4,2,16,2,64,64]{5,4,3,1,0,2:T(8,128)(2,1)}) %all-gather.5.cloned.1.call-update) | async-done | bytes 2097168 | tf_op jit(solution)/shard_map/all_gather | solution.py:77
  465.4 6.9 %copy.74 = bf16[4,2,16,2,64,64]{5,2,3,1,0,4:T(8,128)(2,1)} copy(bf16[4,2,16,2,64,64]{5,4,3,1,0,2:T(8,128)(2,1)} %all-gather.5.cloned.1.call-done) | data formatting | bytes 4194304 | tf_op jit(solution)/shard_map/all_gather | solution.py:77
  472.3 7.6 %reshape.298 = bf16[16,2,32768]{2,1,0:T(2,128)(2,1)} reshape(bf16[64,4,2,2,16,64]{5,4,3,2,1,0:T(8,128)(2,1)} %bitcast.161) | data formatting | bytes 4194304
  479.9 7.3 %all-to-all-start = ((bf16[16,2,32768]{2,1,0:T(2,128)(2,1)}), bf16[16,2,32768]{2,1,0:T(2,128)(2,1)S(1)}, u32[]{:S(2)}, u32[]{:S(2)}) async-start(bf16[16,2,32768]{2,1,0:T(2,128)(2,1)} %reshape.298), calls=%async_computation.1 | async-start | bytes 4194304 | tf_op jit(solution)/shard_map/all_to_all | solution.py:78
  492.3 3.4 multiply_reduce_fusion
  495.8 18.6 %all-to-all-done = bf16[16,2,32768]{2,1,0:T(2,128)(2,1)S(1)} async-done(((bf16[16,2,32768]{2,1,0:T(2,128)(2,1)}), bf16[16,2,32768]{2,1,0:T(2,128)(2,1)S(1)}, u32[]{:S(2)}, u32[]{:S(2)}) %all-to-all-start) | async-done | bytes 2097184 | tf_op jit(solution)/shard_map/all_to_all | solution.py:78
  514.4 5.0 reshape.299
  519.4 3.4 copy.30
  523.8 70.8 %all-reduce = bf16[1,2,64,64]{3,2,1,0:T(8,128)(2,1)S(1)} all-reduce(bf16[1,2,64,64]{3,2,1,0:T(8,128)(2,1)S(1)} %fusion.26), channel_id=3, replica_groups=mesh['mode'=16,'site'=16] {'mode'}, use_global_device_ids=true, to_apply=%region_4.5.clone | all-reduce | flops 8192 | bytes 32768
  (52 shorter events, 14.7 us)
Async XLA Ops:
  6.5 4.1 copy-start
  6.5 68.9 %all-gather.3.cloned.1.call-start = ((), (), s32[]{:S(2)}) async-start(), calls=%async_computation.2 | async-start | bytes 5640192 | tf_op jit(solution)/shard_map/all_gather | solution.py:30
  8.6 229.5 %all-reduce.3.cloned.1.call-start = ((), (), s32[]{:S(2)}) async-start(), calls=%async_computation.3 | async-start | bytes 1048576 | tf_op jit(solution)/shard_map/psum | solution.py:53
  101.1 0.8 copy-start.2
  101.9 261.8 %reduce-scatter.3.cloned.1.call-start = ((), (), s32[]{:S(2)}) async-start(), calls=%async_computation.4 | async-start | bytes 8912896 | tf_op jit(solution)/shard_map/reduce_scatter | solution.py:71
  253.9 211.5 %all-gather.5.cloned.1.call-start = ((), (), s32[]{:S(2)}) async-start(), calls=%async_computation.5 | async-start | bytes 4456448 | tf_op jit(solution)/shard_map/all_gather | solution.py:77
  472.3 14.9 %copy-start.5 = (u32[256]{0:T(256)S(1)}, u32[256]{0:T(256)}, u32[]{:S(2)}) copy-start(u32[256]{0:T(256)} %constant.88) | copy-start | bytes 3076
  472.3 16.1 %copy-start.3 = (s32[1,2]{1,0:T(1,128)S(1)}, s32[1,2]{1,0:T(1,128)}, u32[]{:S(2)}) copy-start(s32[1,2]{1,0:T(1,128)} %param.13) | copy-start | bytes 28
  472.3 17.3 %copy-start.4 = (s32[1,2]{1,0:T(1,128)S(1)}, s32[1,2]{1,0:T(1,128)}, u32[]{:S(2)}) copy-start(s32[1,2]{1,0:T(1,128)} %param.12) | copy-start | bytes 28
  479.9 34.5 %all-to-all-start = ((bf16[16,2,32768]{2,1,0:T(2,128)(2,1)}), bf16[16,2,32768]{2,1,0:T(2,128)(2,1)S(1)}, u32[]{:S(2)}, u32[]{:S(2)}) async-start(bf16[16,2,32768]{2,1,0:T(2,128)(2,1)} %reshape.298), calls=%async_computation.1 | async-start | bytes 4194304 | tf_op jit(solution)/shard_map/all_to_all | solution.py:78
  519.4 75.7 %copy-start.1 = (bf16[2,16,64,64]{3,2,1,0:T(8,128)(2,1)S(1)}, bf16[2,16,64,64]{3,2,1,0:T(8,128)(2,1)}, u32[]{:S(2)}) copy-start(bf16[2,16,64,64]{3,2,1,0:T(8,128)(2,1)} %param.9) | copy-start | bytes 786436
Sparse Core Ops, SparseCore 0:
  10.0 65.4 all-gather.2
  102.0 136.0 all-reduce.2
  254.0 109.6 reduce-scatter.2
  365.6 99.7 all-gather.4
where the time goes:
time: 602 us
  waiting for transfers between devices  428 us (71%)
  blocking collectives  70.8 us (12%)
  local copies, waits for them, and re-layouts  45.4 us (8%)
  other arithmetic  21.7 us (4%)
  between operations  13.9 us (2%)
  matrix products  13.8 us (2%)
  starting transfers between devices  7.58 us (1%)
    psum x1, waiting for transfers between devices, body(): totals = lax.psum(partial_sums, 'site')  136 us
    reduce_scatter x1, waiting for transfers between devices, body(): lax.psum_scatter(jnp.einsum('tcmi,itcpjk->mtcpjk', cols_sel, second, pref...  110 us
    all_gather x1, waiting for transfers between devices, body(): all_blocks = lax.all_gather(own_blocks, 'site', axis=2, tiled=True)  99.9 us
    unnamed x1, blocking collectives  70.8 us
    all_gather x1, waiting for transfers between devices, body(): gathered = lax.all_gather(eigvecs, 'mode', axis=1, tiled=True)  64.4 us
    unnamed x17, local copies, waits for them, and re-layouts  21.4 us
    all_to_all x1, waiting for transfers between devices, body(): lax.all_to_all(all_blocks, 'mode', split_axis=4, concat_axis=0, tiled=True)  18.6 us
  transfers between devices with their start and end apart: 5, of which 5 were waited for; matrix products, arithmetic and copies ran while one was open for 2% of the time, Pallas kernels for 0%

commit v1 on v0

--- a/solution.py
+++ b/solution.py
@@ -4,6 +4,12 @@
 from jax.sharding import PartitionSpec as P
 
 LAT = 48
+
+
+def add_all(array, axis):
+    parts = lax.all_gather(array, axis, axis=0, tiled=False)
+    acc = parts.sum(axis=0)
+    return acc
 
 
 def hartley(momenta, glob):
@@ -50,7 +56,7 @@
         return product.reshape(mode_dev, nmode, nmom, nmode)
 
     partial_sums = lax.map(triplet_part, gathered)
-    totals = lax.psum(partial_sums, "site")
+    totals = add_all(partial_sums, "site")
     triplet = (totals * float(LAT) ** (-1.5)).astype(jnp.bfloat16)
     comb_ids = jnp.arange(ncomb, dtype=jnp.int32)
     mom_ids = jnp.arange(nmom, dtype=jnp.int32)

time: 602 us -> 651 us (1.081)
  waiting for transfers between devices: 428 us -> 474 us
    all_gather x0 -> x1, waiting for transfers between devices: none -> 182 us  [add_all(): parts = lax.all_gather(array, axis, axis=0, tiled=False)]
    psum x1 -> x0, waiting for transfers between devices: 136 us -> none  [body(): totals = lax.psum(partial_sums, 'site')]
where the time goes in v1:
time: 651 us; the launch traced here: 650 us
  waiting for transfers between devices  474 us (73%)
  blocking collectives  70.8 us (11%)
  local copies, waits for them, and re-layouts  44.7 us (7%)
  other arithmetic  26.2 us (4%)
  between operations  13.9 us (2%)
  matrix products  12.8 us (2%)
  starting transfers between devices  7.58 us (1%)
    all_gather x1, waiting for transfers between devices, add_all(): parts = lax.all_gather(array, axis, axis=0, tiled=False)  182 us
    reduce_scatter x1, waiting for transfers between devices, body(): lax.psum_scatter(jnp.einsum('tcmi,itcpjk->mtcpjk', cols_sel, second, pref...  108 us
    all_gather x1, waiting for transfers between devices, body(): all_blocks = lax.all_gather(own_blocks, 'site', axis=2, tiled=True)  100 us
    unnamed x1, blocking collectives  70.8 us
    all_gather x1, waiting for transfers between devices, body(): gathered = lax.all_gather(eigvecs, 'mode', axis=1, tiled=True)  65.7 us
    unnamed x17, local copies, waits for them, and re-layouts  21.4 us
    all_to_all x1, waiting for transfers between devices, body(): lax.all_to_all(all_blocks, 'mode', split_axis=4, concat_axis=0, tiled=True)  18.6 us
  transfers between devices with their start and end apart: 5, of which 5 were waited for; matrix products, arithmetic and copies ran while one was open for 2% of the time, Pallas kernels for 0%

profile of v1, /device:TPU:38, one launch (start us, length us, event | category | flops | bytes accessed | tf_op | source)
XLA Modules:
  0.0 650.4 jit_solution(5910338777041025295)
XLA Ops:
  6.5 2.0 copy.22
  9.8 65.7 %all-gather.5.cloned.1.call-done = bf16[2,64,3,6912]{3,0,2,1:T(2,128)(2,1)} async-done(((bf16[2,4,3,6912]{3,0,2,1:T(2,128)(2,1)}), bf16[2,64,3,6912]{3,0,2,1:T(2,128)(2,1)}) %all-gather.5.cloned.1.call-update) | async-done | bytes 5308432 | tf_op jit(solution)/shard_map/all_gather | solution.py:36
  75.5 5.4 copy.23
  80.9 20.2 %while.13 = (s32[]{:T(128)}, f32[2,4,64,2,64]{4,2,3,1,0:T(8,128)S(1)}, bf16[2,64,3,6912]{3,1,2,0:T(8,128)(2,1)}, s32[]{:T(128)}, s32[6912]{0:T(1024)S(1)}, /*ind...) while((s32[]{:T(128)}, ...), condition=%wide.region_1.2_spmd.clone, body=%wide.region_0.1_spmd.clone.sunk | while | flops 1418867712 | bytes 57853072 | solution.py:58
  80.9 2.4 dynamic-slice_convert_fusion.3
  83.8 3.2 subtract_convert_fusion.4
  88.0 3.0 fusion.62
  91.0 2.4 dynamic-slice_convert_fusion.3
  93.9 3.2 subtract_convert_fusion.4
  98.1 3.0 fusion.62
  103.2 181.8 %all-gather.9.cloned.1.call-done = f32[32,4,64,2,64]{4,2,3,1,0:T(8,128)} async-done(((f32[2,4,64,2,64]{4,2,3,1,0:T(8,128)}), f32[32,4,64,2,64]{4,2,3,1,0:T(8,128)}) %all-gather.9.cloned.1.call-update) | async-done | bytes 4194320 | tf_op jit(solution)/shard_map/all_gather | solution.py:10
  285.0 4.4 reduce_sum.9
  290.2 4.9 convolution_bitcast_fusion
  295.1 9.1 %copy.26 = f32[64,2,1,2,64,64]{5,4,3,2,1,0:T(8,128)} copy(f32[64,2,1,2,64,64]{0,5,4,3,1,2:T(8,128)} %convolution_bitcast_fusion) | data formatting | bytes 8388608 | tf_op jit(solution)/shard_map/tcmi,itcpjk->mtcpjk/transpose | solution.py:78
  304.3 108.2 %reduce-scatter.3.cloned.1.call-done = f32[4,2,1,2,64,64]{5,4,3,2,1,0:T(8,128)} async-done(((f32[64,2,1,2,64,64]{5,4,3,2,1,0:T(8,128)}), f32[4,2,1,2,64,64]{5,4,3,2,1,0:T(8,128)}) %reduce-scatter.3.cloned.1.call-update) | async-done | bytes 262160 | tf_op jit(solution)/shard_map/reduce_scatter | solution.py:77
  414.3 100.0 %all-gather.7.cloned.1.call-done = bf16[4,2,16,2,64,64]{5,4,3,1,0,2:T(8,128)(2,1)} async-done(((bf16[4,2,1,2,64,64]{5,4,3,1,0,2:T(8,128)(2,1)}), bf16[4,2,16,2,64,64]{5,4,3,1,0,2:T(8,128)(2,1)}) %all-gather.7.cloned.1.call-update) | async-done | bytes 2097168 | tf_op jit(solution)/shard_map/all_gather | solution.py:83
  514.3 6.9 %copy.74 = bf16[4,2,16,2,64,64]{5,2,3,1,0,4:T(8,128)(2,1)} copy(bf16[4,2,16,2,64,64]{5,4,3,1,0,2:T(8,128)(2,1)} %all-gather.7.cloned.1.call-done) | data formatting | bytes 4194304 | tf_op jit(solution)/shard_map/all_gather | solution.py:83
  521.2 7.6 %reshape.299 = bf16[16,2,32768]{2,1,0:T(2,128)(2,1)} reshape(bf16[64,4,2,2,16,64]{5,4,3,2,1,0:T(8,128)(2,1)} %bitcast.162) | data formatting | bytes 4194304
  528.7 7.3 %all-to-all-start = ((bf16[16,2,32768]{2,1,0:T(2,128)(2,1)}), bf16[16,2,32768]{2,1,0:T(2,128)(2,1)S(1)}, u32[]{:S(2)}, u32[]{:S(2)}) async-start(bf16[16,2,32768]{2,1,0:T(2,128)(2,1)} %reshape.299), calls=%async_computation.1 | async-start | bytes 4194304 | tf_op jit(solution)/shard_map/all_to_all | solution.py:84
  541.2 3.4 multiply_reduce_fusion
  544.7 18.6 %all-to-all-done = bf16[16,2,32768]{2,1,0:T(2,128)(2,1)S(1)} async-done(((bf16[16,2,32768]{2,1,0:T(2,128)(2,1)}), bf16[16,2,32768]{2,1,0:T(2,128)(2,1)S(1)}, u32[]{:S(2)}, u32[]{:S(2)}) %all-to-all-start) | async-done | bytes 2097184 | tf_op jit(solution)/shard_map/all_to_all | solution.py:84
  563.3 5.0 reshape.300
  568.2 3.3 copy.30
  572.5 70.8 %all-reduce = bf16[1,2,64,64]{3,2,1,0:T(8,128)(2,1)S(1)} all-reduce(bf16[1,2,64,64]{3,2,1,0:T(8,128)(2,1)S(1)} %fusion.26), channel_id=4, replica_groups=mesh['mode'=16,'site'=16] {'mode'}, use_global_device_ids=true, to_apply=%region_4.5.clone | all-reduce | flops 8192 | bytes 32768
  (53 shorter events, 14.8 us)
Async XLA Ops:
  6.5 95.8 %copy-start = (bf16[2,16,64,64]{3,2,1,0:T(8,128)(2,1)S(1)}, bf16[2,16,64,64]{3,2,1,0:T(8,128)(2,1)}, u32[]{:S(2)}) copy-start(bf16[2,16,64,64]{3,2,1,0:T(8,128)(2,1)} %param.9) | copy-start | bytes 786436
  6.5 68.9 %all-gather.5.cloned.1.call-start = ((), (), s32[]{:S(2)}) async-start(), calls=%async_computation.2 | async-start | bytes 5640192 | tf_op jit(solution)/shard_map/all_gather | solution.py:36
  8.6 276.4 %all-gather.9.cloned.1.call-start = ((), (), s32[]{:S(2)}) async-start(), calls=%async_computation.5 | async-start | bytes 8912896 | tf_op jit(solution)/shard_map/all_gather | solution.py:10
  80.9 21.3 %copy-start.2 = (s32[16,3]{0,1:T(4,128)S(1)}, s32[16,3]{0,1:T(4,128)}, u32[]{:S(2)}) copy-start(s32[16,3]{0,1:T(4,128)} %param.11) | copy-start | bytes 580
  101.1 0.8 copy-start.1
  101.9 310.6 %reduce-scatter.3.cloned.1.call-start = ((), (), s32[]{:S(2)}) async-start(), calls=%async_computation.3 | async-start | bytes 8912896 | tf_op jit(solution)/shard_map/reduce_scatter | solution.py:77
  304.2 210.0 %all-gather.7.cloned.1.call-start = ((), (), s32[]{:S(2)}) async-start(), calls=%async_computation.4 | async-start | bytes 4456448 | tf_op jit(solution)/shard_map/all_gather | solution.py:83
  521.1 14.9 %copy-start.5 = (u32[256]{0:T(256)S(1)}, u32[256]{0:T(256)}, u32[]{:S(2)}) copy-start(u32[256]{0:T(256)} %constant.89) | copy-start | bytes 3076
  521.1 16.1 %copy-start.3 = (s32[1,2]{1,0:T(1,128)S(1)}, s32[1,2]{1,0:T(1,128)}, u32[]{:S(2)}) copy-start(s32[1,2]{1,0:T(1,128)} %param.13) | copy-start | bytes 28
  521.1 17.3 %copy-start.4 = (s32[1,2]{1,0:T(1,128)S(1)}, s32[1,2]{1,0:T(1,128)}, u32[]{:S(2)}) copy-start(s32[1,2]{1,0:T(1,128)} %param.12) | copy-start | bytes 28
  528.7 34.5 %all-to-all-start = ((bf16[16,2,32768]{2,1,0:T(2,128)(2,1)}), bf16[16,2,32768]{2,1,0:T(2,128)(2,1)S(1)}, u32[]{:S(2)}, u32[]{:S(2)}) async-start(bf16[16,2,32768]{2,1,0:T(2,128)(2,1)} %reshape.299), calls=%async_computation.1 | async-start | bytes 4194304 | tf_op jit(solution)/shard_map/all_to_all | solution.py:84
Sparse Core Ops, SparseCore 0:
  10.0 65.4 all-gather.4
  102.0 182.9 all-gather.8
  304.4 108.1 reduce-scatter.2
  414.5 99.7 all-gather.6
